TPU v7x, 32 devices: a whole 2x2x4 slice. The times are simulated.
32 devices in a mesh: gx: 4 (over y, core), gz: 4 (over z), grp: 2 (over x).
Axes of the slice: x: 2, y: 2, z: 4, core: 2. Of those that a mesh axis runs over, the one named last changes fastest.
Arguments:
- velocity: float32 [3, 3, 512, 2048], P(None, None, ('gz', 'grp'), 'gx'), may hold values from -5 to 5
- slab_average_downflow_speed: float32 [3], replicated, may hold values from 0.5 to 2
- mean_shear: float32 [3], replicated, may hold values from -2 to 2
- mode_counts: int32 [3, 2], replicated, may hold values from 64 to 128
Outputs:
- advanced: float32 [3, 3, 512, 2048], P(None, None, ('gz', 'grp'), 'gx')
- stress: float32 [6, 3, 512, 2048], P(None, None, ('gz', 'grp'), 'gx')
All inputs are finite; a program needn't handle non-finite values.
Results may differ from a plain program's by a relative error of at most 0.00015.
Values sent between devices are 32-bit elements; how exact they have to be, the bound alone decides.
A program may use at most 64 MiB of HBM per device.

v0:
```python
import math
import jax
import jax.numpy as jnp
from jax import lax
from jax.sharding import PartitionSpec as P

NX = 2048
NZ = 512
MODES = 256
molecular_diffusivity = 0.4
time_step = 0.2
highest = lax.Precision.HIGHEST
pair_first = (0, 0, 0, 1, 1, 2)
pair_second = (0, 1, 2, 1, 2, 2)


def with_halo(cells, sides, width):
    for axis, dim in sides:
        count = lax.axis_size(axis)
        head = lax.slice_in_dim(cells, 0, width, axis=dim)
        tail = lax.slice_in_dim(cells, cells.shape[dim] - width, cells.shape[dim], axis=dim)
        cells = jnp.concatenate(
            [
                lax.ppermute(tail, axis, [(i, (i + 1) % count) for i in range(count)]),
                cells,
                lax.ppermute(head, axis, [((i + 1) % count, i) for i in range(count)]),
            ],
            axis=dim,
        )
    return cells


def wave_numbers(modes):
    column = jnp.arange(modes, dtype=jnp.int32)
    half_modes = modes // 2
    return jnp.where(column < half_modes, column, column - half_modes + 1)


def wave_table(positions, length, modes):
    column = jnp.arange(modes, dtype=jnp.int32)
    numbers = wave_numbers(modes)
    phase_int = positions[:, None] * numbers[None, :] % length
    angles = phase_int.astype(jnp.float32) * jnp.float32(2.0 * math.pi / length)
    return jnp.where(column[None, :] < modes // 2, jnp.cos(angles), jnp.sin(angles))


def mode_weights(length, modes):
    column = jnp.arange(modes, dtype=jnp.int32)
    return jnp.where(column == 0, jnp.float32(1.0 / length), jnp.float32(2.0 / length))


def tendency_from(
    middle_entry,
    east_cells,
    west_cells,
    north_cells,
    south_cells,
    slab_average_downflow_speed,
    mean_shear,
):
    downflow_derivative_field = (east_cells - west_cells) * 0.5
    crossflow_derivative_field = (north_cells - south_cells) * 0.5
    diffusion_contribution = (
        east_cells + west_cells + north_cells + south_cells - 4.0 * middle_entry
    )
    holding_slab = slab_average_downflow_speed[:, None, None] + middle_entry[0]
    advanced_state = (
        -holding_slab[None] * downflow_derivative_field
        - middle_entry[2][None] * crossflow_derivative_field
        + molecular_diffusivity * diffusion_contribution
    )
    shear_term = mean_shear[:, None, None] * middle_entry[1]
    return jnp.concatenate([advanced_state[0:1] - shear_term[None], advanced_state[1:]], axis=0)


def runge_kutta(velocity, rate):
    first = velocity + time_step * rate(velocity)
    second = 0.75 * velocity + 0.25 * (first + time_step * rate(first))
    return velocity / 3.0 + 2.0 / 3.0 * (second + time_step * rate(second))


def with_products(components):
    products = [
        components[first_idx] * components[second_idx]
        for first_idx, second_idx in zip(pair_first, pair_second)
    ]
    return jnp.concatenate([components, jnp.stack(products)], axis=0)


def padded_rate(padded, slab_average_downflow_speed, mean_shear):
    return tendency_from(
        padded[:, :, 1:-1, 1:-1],
        padded[:, :, 1:-1, 2:],
        padded[:, :, 1:-1, :-2],
        padded[:, :, 2:, 1:-1],
        padded[:, :, :-2, 1:-1],
        slab_average_downflow_speed,
        mean_shear,
    )


def local(velocity, slab_average_downflow_speed, mean_shear, mode_counts):
    plane_count = velocity.shape[1]
    cells_z = velocity.shape[2]
    cells_x = velocity.shape[3]

    def rate(field):
        padded = with_halo(field, ((("gz", "grp"), 2), ("gx", 3)), 1)
        return padded_rate(padded, slab_average_downflow_speed, mean_shear)

    advanced = runge_kutta(velocity, rate)
    streamwise_devices = lax.axis_size("gx")
    spanwise_devices = lax.axis_size(("gz", "grp"))
    modes_x_local = MODES // streamwise_devices
    modes_z_local = MODES // spanwise_devices
    x_positions = lax.axis_index("gx") * cells_x + jnp.arange(cells_x, dtype=jnp.int32)
    z_positions = lax.axis_index(("gz", "grp")) * cells_z + jnp.arange(cells_z, dtype=jnp.int32)
    synth_x = wave_table(x_positions, NX, MODES)
    synth_z = wave_table(z_positions, NZ, MODES)
    tile_fields = with_products(advanced)
    analysis_x = synth_x * mode_weights(NX, MODES)[None, :]
    columns = analysis_x
    streamwise = lax.psum_scatter(
        jnp.einsum("fpzx,xm->mfpz", tile_fields, columns, precision=highest),
        "gx",
        scatter_dimension=0,
        tiled=True,
    )
    line_count = modes_x_local * 9 * plane_count
    per_device = -(-line_count // spanwise_devices)
    padded_count = per_device * spanwise_devices
    flat_lines = streamwise.reshape(line_count, cells_z)
    flat_lines = jnp.pad(flat_lines, ((0, padded_count - line_count), (0, 0)))
    zlines = lax.all_to_all(flat_lines, ("gz", "grp"), split_axis=0, concat_axis=1, tiled=True)
    whole_z = (
        wave_table(jnp.arange(NZ, dtype=jnp.int32), NZ, MODES) * mode_weights(NZ, MODES)[None, :]
    )
    zcoeffs = jnp.einsum("iz,zn->ni", zlines, whole_z, precision=highest)
    gathered = lax.all_to_all(zcoeffs, ("gz", "grp"), split_axis=0, concat_axis=1, tiled=True)
    spectral = gathered[:, :line_count].reshape(modes_z_local, modes_x_local, 9, plane_count)
    numbers = wave_numbers(MODES)
    z_modes = lax.axis_index(("gz", "grp")) * modes_z_local + jnp.arange(
        modes_z_local, dtype=jnp.int32
    )
    x_modes = lax.axis_index("gx") * modes_x_local + jnp.arange(modes_x_local, dtype=jnp.int32)
    keep_z = jnp.take(numbers, z_modes)[:, None] <= mode_counts[:, 1][None, :]
    keep_x = jnp.take(numbers, x_modes)[:, None] <= mode_counts[:, 0][None, :]
    keep = (keep_z[:, None, :] & keep_x[None, :, :]).astype(jnp.float32)
    spectral = spectral * keep[:, :, None, :]
    columns = synth_z
    partial_sum = jnp.einsum(
        "nmfp,zn->mfpz",
        lax.all_gather(spectral, ("gz", "grp"), axis=0, tiled=True),
        columns,
        precision=highest,
    )
    columns = synth_x
    filtered = jnp.einsum(
        "mfpz,xm->fpzx",
        lax.all_gather(partial_sum, "gx", axis=0, tiled=True),
        columns,
        precision=highest,
    )
    stresses = [
        filtered[3 + index] - filtered[first_idx] * filtered[second_idx]
        for index, (first_idx, second_idx) in enumerate(zip(pair_first, pair_second))
    ]
    return (advanced, jnp.stack(stresses))


def solution(mesh):
    return jax.shard_map(
        local,
        mesh=mesh,
        in_specs=(P(None, None, ("gz", "grp"), "gx"), P(), P(), P()),
        out_specs=(P(None, None, ("gz", "grp"), "gx"), P(None, None, ("gz", "grp"), "gx")),
        check_vma=False,
    )
```

profile of v0, /device:TPU:0, one launch (start us, length us, event | category | flops | bytes accessed | tf_op | source)
XLA Modules:
  0.0 298.7 jit_solution(3138307370650989517)
XLA Ops:
  8.3 3.0 %collective-permute-start = (f32[3,3,1,512]{3,2,1,0:T(1,128)S(1)}, f32[3,3,1,512]{3,2,1,0:T(1,128)S(1)}, u32[]{:S(2)}, u32[]{:S(2)}) collective-permute-start(f32[3,3,1,512]{3,2,1,0:T(1,128)S(1)} %get-tuple-element.20), channel_id=1, source_target_pairs={{0,1},{1,2},{2,3},{3,4},{4,5},{5,6},{6,7},{7,0},{8,9},{9,10},{10,1... | collective-permute-start | bytes 55304 | tf_op jit(solution)/shard_map/ppermute | solution.py:24
  11.3 3.1 %collective-permute-start.1 = (f32[3,3,1,512]{3,2,1,0:T(1,128)S(1)}, f32[3,3,1,512]{3,2,1,0:T(1,128)S(1)}, u32[]{:S(2)}, u32[]{:S(2)}) collective-permute-start(f32[3,3,1,512]{3,2,1,0:T(1,128)S(1)} %get-tuple-element.21), channel_id=1, source_target_pairs={{1,0},{2,1},{3,2},{4,3},{5,4},{6,5},{7,6},{0,7},{9,8},{10,9},{11,1... | collective-permute-start | bytes 55304 | tf_op jit(solution)/shard_map/ppermute | solution.py:26
  14.4 1.2 multiply_bitcast_fusion.1
  16.4 1.7 collective-permute-start.2
  18.1 6.3 %collective-permute-done.3 = f32[3,3,66,1]{3,2,1,0:T(8,128)S(1)} collective-permute-done((f32[3,3,66,1]{3,2,1,0:T(8,128)S(1)}, f32[3,3,66,1]{3,2,1,0:T(8,128)S(1)}, u32[]{:S(2)}, u32[]{:S(2)}) %collective-permute-start.3) | collective-permute-done | bytes 2408 | tf_op jit(solution)/shard_map/ppermute | solution.py:24
  24.5 1.2 collective-permute-done.2
  28.0 1.3 collective-permute-start.4
  29.3 3.5 %collective-permute-start.5 = (f32[3,3,1,512]{3,2,1,0:T(1,128)S(1)}, f32[3,3,1,512]{3,2,1,0:T(1,128)S(1)}, u32[]{:S(2)}, u32[]{:S(2)}) collective-permute-start(f32[3,3,1,512]{3,2,1,0:T(1,128)S(1)} %get-tuple-element.17), channel_id=1, source_target_pairs={{1,0},{2,1},{3,2},{4,3},{5,4},{6,5},{7,6},{0,7},{9,8},{10,9},{11,1... | collective-permute-start | bytes 55304 | tf_op jit(solution)/shard_map/ppermute | solution.py:26
  32.8 1.8 collective-permute-done.4
  35.0 1.7 collective-permute-start.6
  36.7 6.2 %collective-permute-done.7 = f32[3,3,66,1]{3,2,1,0:T(8,128)S(1)} collective-permute-done((f32[3,3,66,1]{3,2,1,0:T(8,128)S(1)}, f32[3,3,66,1]{3,2,1,0:T(8,128)S(1)}, u32[]{:S(2)}, u32[]{:S(2)}) %collective-permute-start.7) | collective-permute-done | bytes 2408 | tf_op jit(solution)/shard_map/ppermute | solution.py:24
  43.0 1.2 collective-permute-done.6
  44.2 1.2 multiply_add_fusion.1
  46.1 4.8 %collective-permute-start.9 = (f32[3,3,1,512]{3,2,1,0:T(1,128)S(1)}, f32[3,3,1,512]{3,2,1,0:T(1,128)S(1)}, u32[]{:S(2)}, u32[]{:S(2)}) collective-permute-start(f32[3,3,1,512]{3,2,1,0:T(1,128)S(1)} %get-tuple-element.13), channel_id=1, source_target_pairs={{1,0},{2,1},{3,2},{4,3},{5,4},{6,5},{7,6},{0,7},{9,8},{10,9},{11,1... | collective-permute-start | bytes 55304 | tf_op jit(solution)/shard_map/ppermute | solution.py:26
  50.9 1.7 collective-permute-done.8
  52.8 1.9 collective-permute-start.10
  54.8 5.7 %collective-permute-done.11 = f32[3,3,66,1]{3,2,1,0:T(8,128)S(1)} collective-permute-done((f32[3,3,66,1]{3,2,1,0:T(8,128)S(1)}, f32[3,3,66,1]{3,2,1,0:T(8,128)S(1)}, u32[]{:S(2)}, u32[]{:S(2)}) %collective-permute-start.11) | collective-permute-done | bytes 2408 | tf_op jit(solution)/shard_map/ppermute | solution.py:24
  60.5 1.9 collective-permute-done.10
  65.3 15.6 %fusion.16 = f32[256,9,3,64]{3,0,2,1:T(8,128)} fusion(f32[9,3,64,512]{3,2,1,0:T(8,128)S(1)} %multiply_dynamic-update-slice_fusion, f32[256]{0:T(256)S(1)} %compare_select_fusion.4, s32[256]{0:T(256)S(1)} %add_select_fusion.4, s32[512]{0:T(512)S(1)} %iota_add_fusion, pred[256]{0:T(512)(128)(4,1)S(1)} %iota_compare_fusion), kind=kOutput, calls=%fused_computation.57 | convolution fusion | flops 2720006144 | bytes 5312768 | tf_op jit(solution)/shard_map/fpzx,xm->mfpz/dot_general | solution.py:124
  82.5 40.7 %reduce-scatter.2.cloned.1.call-done = f32[64,9,3,64]{3,0,2,1:T(8,128)} async-done(((f32[256,9,3,64]{3,0,2,1:T(8,128)}), f32[64,9,3,64]{3,0,2,1:T(8,128)}) %reduce-scatter.2.cloned.1.call-update) | async-done | bytes 442384 | tf_op jit(solution)/shard_map/reduce_scatter | solution.py:123
  123.2 1.8 copy.13
  126.5 5.5 %all-to-all-start = ((f32[8,216,64]{1,2,0:T(8,128)}), f32[8,216,64]{1,2,0:T(8,128)S(1)}, u32[]{:S(2)}, u32[]{:S(2)}) async-start(f32[8,216,64]{1,2,0:T(8,128)} %copy.14), calls=%async_computation.1 | async-start | bytes 1048576 | tf_op jit(solution)/shard_map/all_to_all | solution.py:134
  132.2 14.2 %all-to-all-done = f32[8,216,64]{1,2,0:T(8,128)S(1)} async-done(((f32[8,216,64]{1,2,0:T(8,128)}), f32[8,216,64]{1,2,0:T(8,128)S(1)}, u32[]{:S(2)}, u32[]{:S(2)}) %all-to-all-start) | async-done | bytes 442400 | tf_op jit(solution)/shard_map/all_to_all | solution.py:134
  146.4 4.6 %fusion.18 = f32[8,32,216]{2,1,0:T(8,128)} fusion(f32[216,512,1]{0,1,2:T(8,128)S(1)} %bitcast.48, f32[8,32]{1,0:T(8,128)S(1)} %fusion.76, s32[8,32]{1,0:T(8,128)S(1)} %add_select_fusion.3, pred[8,32]{1,0:T(8,128)(4,1)S(1)} %fusion.75), kind=kOutput, calls=%fused_computation.59 | convolution fusion | flops 341835776 | bytes 665856 | tf_op jit(solution)/shard_map/iz,zn->ni/dot_general | solution.py:138
  151.0 3.6 %all-to-all-start.1 = ((f32[8,32,216]{2,1,0:T(8,128)}), f32[8,32,216]{2,1,0:T(8,128)S(1)}, u32[]{:S(2)}, u32[]{:S(2)}) async-start(f32[8,32,216]{2,1,0:T(8,128)} %fusion.18), calls=%async_computation.2 | async-start | bytes 524288 | tf_op jit(solution)/shard_map/all_to_all | solution.py:139
  154.9 8.7 %all-to-all-done.1 = f32[8,32,216]{2,1,0:T(8,128)S(1)} async-done(((f32[8,32,216]{2,1,0:T(8,128)}), f32[8,32,216]{2,1,0:T(8,128)S(1)}, u32[]{:S(2)}, u32[]{:S(2)}) %all-to-all-start.1) | async-done | bytes 221216 | tf_op jit(solution)/shard_map/all_to_all | solution.py:139
  166.2 62.4 %all-gather.3.cloned.1.call-done = f32[256,64,9,3]{1,0,3,2:T(8,128)} async-done(((f32[32,64,9,3]{1,0,3,2:T(8,128)}), f32[256,64,9,3]{1,0,3,2:T(8,128)}) %all-gather.3.cloned.1.call-update) | async-done | bytes 1769488 | tf_op jit(solution)/shard_map/all_gather | solution.py:153
  228.6 7.8 %fusion.58 = f32[64,9,3,64]{3,0,2,1:T(8,128)S(1)} fusion(f32[256,64,9,3]{1,0,3,2:T(8,128)} %all-gather.3.cloned.1.call-done, s32[256]{0:T(256)S(1)} %add_select_fusion.4, s32[64]{0:T(128)S(1)} %iota_add_fusion.1, pred[256]{0:T(512)(128)(4,1)S(1)} %iota_compare_fusion), kind=kOutput, calls=%fused_computation.133 | convolution fusion | flops 339984384 | bytes 2213376 | tf_op jit(solution)/shard_map/nmfp,zn->mfpz/dot_general | solution.py:151
  236.4 1.6 copy.18
  238.0 36.3 %all-gather.5.cloned.1.call-done = f32[256,9,3,64]{3,2,1,0:T(4,128)} async-done(((f32[64,9,3,64]{3,2,1,0:T(4,128)}), f32[256,9,3,64]{3,2,1,0:T(4,128)}) %all-gather.5.cloned.1.call-update) | async-done | bytes 1769488 | tf_op jit(solution)/shard_map/all_gather | solution.py:160
  274.4 15.7 %fusion = f32[9,3,64,512]{3,2,1,0:T(8,128)S(1)} fusion(f32[256,9,3,64]{3,2,1,0:T(4,128)} %all-gather.5.cloned.1.call-done, s32[256]{0:T(256)S(1)} %add_select_fusion.4, s32[512]{0:T(512)S(1)} %iota_add_fusion, pred[256]{0:T(512)(128)(4,1)S(1)} %iota_compare_fusion), kind=kOutput, calls=%fused_computation.2 | convolution fusion | flops 2719875072 | bytes 5311744 | tf_op jit(solution)/shard_map/mfpz,xm->fpzx/dot_general | solution.py:158
  290.6 1.4 copy-done.2
  (81 shorter events, 14.7 us)
Async XLA Ops:
  7.2 9.0 %copy-start = (f32[3,3,64,512]{3,2,1,0:T(8,128)S(1)}, f32[3,3,64,512]{3,2,1,0:T(8,128)}, u32[]{:S(2)}) copy-start(f32[3,3,64,512]{3,2,1,0:T(8,128)} %param.4) | copy-start | bytes 3538948
  7.2 116.1 %reduce-scatter.2.cloned.1.call-start = ((), (), s32[]{:S(2)}) async-start(), calls=%async_computation.3 | async-start | bytes 4423680 | tf_op jit(solution)/shard_map/reduce_scatter | solution.py:123
  8.3 7.8 %collective-permute-start = (f32[3,3,1,512]{3,2,1,0:T(1,128)S(1)}, f32[3,3,1,512]{3,2,1,0:T(1,128)S(1)}, u32[]{:S(2)}, u32[]{:S(2)}) collective-permute-start(f32[3,3,1,512]{3,2,1,0:T(1,128)S(1)} %get-tuple-element.20), channel_id=1, source_target_pairs={{0,1},{1,2},{2,3},{3,4},{4,5},{5,6},{6,7},{7,0},{8,9},{9,10},{10,1... | collective-permute-start | bytes 55304 | tf_op jit(solution)/shard_map/ppermute | solution.py:24
  11.3 4.8 %collective-permute-start.1 = (f32[3,3,1,512]{3,2,1,0:T(1,128)S(1)}, f32[3,3,1,512]{3,2,1,0:T(1,128)S(1)}, u32[]{:S(2)}, u32[]{:S(2)}) collective-permute-start(f32[3,3,1,512]{3,2,1,0:T(1,128)S(1)} %get-tuple-element.21), channel_id=1, source_target_pairs={{1,0},{2,1},{3,2},{4,3},{5,4},{6,5},{7,6},{0,7},{9,8},{10,9},{11,1... | collective-permute-start | bytes 55304 | tf_op jit(solution)/shard_map/ppermute | solution.py:26
  16.3 8.1 %collective-permute-start.3 = (f32[3,3,66,1]{3,2,1,0:T(8,128)S(1)}, f32[3,3,66,1]{3,2,1,0:T(8,128)S(1)}, u32[]{:S(2)}, u32[]{:S(2)}) collective-permute-start(f32[3,3,66,1]{3,2,1,0:T(8,128)S(1)} %get-tuple-element.8), channel_id=1, source_target_pairs={{0,8},{8,16},{16,24},{24,0},{1,9},{9,17},{17,25},{25,1},{2,10},{10... | collective-permute-start | bytes 7136 | tf_op jit(solution)/shard_map/ppermute | solution.py:24
  16.4 9.3 %collective-permute-start.2 = (f32[3,3,66,1]{3,2,1,0:T(8,128)S(1)}, f32[3,3,66,1]{3,2,1,0:T(8,128)S(1)}, u32[]{:S(2)}, u32[]{:S(2)}) collective-permute-start(f32[3,3,66,1]{3,2,1,0:T(8,128)S(1)} %get-tuple-element.9), channel_id=1, source_target_pairs={{8,0},{16,8},{24,16},{0,24},{9,1},{17,9},{25,17},{1,25},{10,2},{18... | collective-permute-start | bytes 7136 | tf_op jit(solution)/shard_map/ppermute | solution.py:26
  26.9 0.7 copy-start.4
  27.9 8.7 %copy-start.3 = (f32[3]{0:T(128)S(1)}, f32[3]{0:T(128)}, u32[]{:S(2)}) copy-start(f32[3]{0:T(128)} %param.5) | copy-start | bytes 40
  28.0 6.7 %collective-permute-start.4 = (f32[3,3,1,512]{3,2,1,0:T(1,128)S(1)}, f32[3,3,1,512]{3,2,1,0:T(1,128)S(1)}, u32[]{:S(2)}, u32[]{:S(2)}) collective-permute-start(f32[3,3,1,512]{3,2,1,0:T(1,128)S(1)} %get-tuple-element.16), channel_id=1, source_target_pairs={{0,1},{1,2},{2,3},{3,4},{4,5},{5,6},{6,7},{7,0},{8,9},{9,10},{10,1... | collective-permute-start | bytes 55304 | tf_op jit(solution)/shard_map/ppermute | solution.py:24
  29.3 5.4 %collective-permute-start.5 = (f32[3,3,1,512]{3,2,1,0:T(1,128)S(1)}, f32[3,3,1,512]{3,2,1,0:T(1,128)S(1)}, u32[]{:S(2)}, u32[]{:S(2)}) collective-permute-start(f32[3,3,1,512]{3,2,1,0:T(1,128)S(1)} %get-tuple-element.17), channel_id=1, source_target_pairs={{1,0},{2,1},{3,2},{4,3},{5,4},{6,5},{7,6},{0,7},{9,8},{10,9},{11,1... | collective-permute-start | bytes 55304 | tf_op jit(solution)/shard_map/ppermute | solution.py:26
  34.8 8.1 %collective-permute-start.7 = (f32[3,3,66,1]{3,2,1,0:T(8,128)S(1)}, f32[3,3,66,1]{3,2,1,0:T(8,128)S(1)}, u32[]{:S(2)}, u32[]{:S(2)}) collective-permute-start(f32[3,3,66,1]{3,2,1,0:T(8,128)S(1)} %get-tuple-element.6), channel_id=1, source_target_pairs={{0,8},{8,16},{16,24},{24,0},{1,9},{9,17},{17,25},{25,1},{2,10},{10... | collective-permute-start | bytes 7136 | tf_op jit(solution)/shard_map/ppermute | solution.py:24
  35.0 9.2 %collective-permute-start.6 = (f32[3,3,66,1]{3,2,1,0:T(8,128)S(1)}, f32[3,3,66,1]{3,2,1,0:T(8,128)S(1)}, u32[]{:S(2)}, u32[]{:S(2)}) collective-permute-start(f32[3,3,66,1]{3,2,1,0:T(8,128)S(1)} %get-tuple-element.7), channel_id=1, source_target_pairs={{8,0},{16,8},{24,16},{0,24},{9,1},{17,9},{25,17},{1,25},{10,2},{18... | collective-permute-start | bytes 7136 | tf_op jit(solution)/shard_map/ppermute | solution.py:26
  46.1 6.5 %collective-permute-start.8 = (f32[3,3,1,512]{3,2,1,0:T(1,128)S(1)}, f32[3,3,1,512]{3,2,1,0:T(1,128)S(1)}, u32[]{:S(2)}, u32[]{:S(2)}) collective-permute-start(f32[3,3,1,512]{3,2,1,0:T(1,128)S(1)} %get-tuple-element.12), channel_id=1, source_target_pairs={{0,1},{1,2},{2,3},{3,4},{4,5},{5,6},{6,7},{7,0},{8,9},{9,10},{10,1... | collective-permute-start | bytes 55304 | tf_op jit(solution)/shard_map/ppermute | solution.py:24
  46.1 6.5 %collective-permute-start.9 = (f32[3,3,1,512]{3,2,1,0:T(1,128)S(1)}, f32[3,3,1,512]{3,2,1,0:T(1,128)S(1)}, u32[]{:S(2)}, u32[]{:S(2)}) collective-permute-start(f32[3,3,1,512]{3,2,1,0:T(1,128)S(1)} %get-tuple-element.13), channel_id=1, source_target_pairs={{1,0},{2,1},{3,2},{4,3},{5,4},{6,5},{7,6},{0,7},{9,8},{10,9},{11,1... | collective-permute-start | bytes 55304 | tf_op jit(solution)/shard_map/ppermute | solution.py:26
  52.8 7.7 %collective-permute-start.11 = (f32[3,3,66,1]{3,2,1,0:T(8,128)S(1)}, f32[3,3,66,1]{3,2,1,0:T(8,128)S(1)}, u32[]{:S(2)}, u32[]{:S(2)}) collective-permute-start(f32[3,3,66,1]{3,2,1,0:T(8,128)S(1)} %get-tuple-element.4), channel_id=1, source_target_pairs={{0,8},{8,16},{16,24},{24,0},{1,9},{9,17},{17,25},{25,1},{2,10},{10... | collective-permute-start | bytes 7136 | tf_op jit(solution)/shard_map/ppermute | solution.py:24
  52.8 9.6 %collective-permute-start.10 = (f32[3,3,66,1]{3,2,1,0:T(8,128)S(1)}, f32[3,3,66,1]{3,2,1,0:T(8,128)S(1)}, u32[]{:S(2)}, u32[]{:S(2)}) collective-permute-start(f32[3,3,66,1]{3,2,1,0:T(8,128)S(1)} %get-tuple-element.5), channel_id=1, source_target_pairs={{8,0},{16,8},{24,16},{0,24},{9,1},{17,9},{25,17},{1,25},{10,2},{18... | collective-permute-start | bytes 7136 | tf_op jit(solution)/shard_map/ppermute | solution.py:26
  64.2 1.0 copy-start.1
  125.4 6.7 %copy-start.5 = (s32[3,2]{0,1:T(2,128)S(1)}, s32[3,2]{0,1:T(2,128)}, u32[]{:S(2)}) copy-start(s32[3,2]{0,1:T(2,128)} %param.7) | copy-start | bytes 76
  126.5 19.8 %all-to-all-start = ((f32[8,216,64]{1,2,0:T(8,128)}), f32[8,216,64]{1,2,0:T(8,128)S(1)}, u32[]{:S(2)}, u32[]{:S(2)}) async-start(f32[8,216,64]{1,2,0:T(8,128)} %copy.14), calls=%async_computation.1 | async-start | bytes 1048576 | tf_op jit(solution)/shard_map/all_to_all | solution.py:134
  151.0 12.6 %all-to-all-start.1 = ((f32[8,32,216]{2,1,0:T(8,128)}), f32[8,32,216]{2,1,0:T(8,128)S(1)}, u32[]{:S(2)}, u32[]{:S(2)}) async-start(f32[8,32,216]{2,1,0:T(8,128)} %fusion.18), calls=%async_computation.2 | async-start | bytes 524288 | tf_op jit(solution)/shard_map/all_to_all | solution.py:139
  154.7 73.9 %all-gather.3.cloned.1.call-start = ((), (), s32[]{:S(2)}) async-start(), calls=%async_computation.4 | async-start | bytes 3981312 | tf_op jit(solution)/shard_map/all_gather | solution.py:153
  165.7 108.7 %all-gather.5.cloned.1.call-start = ((), (), s32[]{:S(2)}) async-start(), calls=%async_computation.5 | async-start | bytes 5898240 | tf_op jit(solution)/shard_map/all_gather | solution.py:160
  290.6 1.4 copy-start.2
Sparse Core Ops, SparseCore 0:
  81.0 42.1 reduce-scatter.1
  165.8 62.6 all-gather.2
  238.2 36.1 all-gather.4
where the time goes:
time: 304 us; the launch traced here: 299 us
  waiting for transfers between devices  189 us (62%)
  matrix products  43.8 us (14%)
  starting transfers between devices  31 us (10%)
  between operations  14.4 us (5%)
  local copies, waits for them, and re-layouts  12.2 us (4%)
  other arithmetic  8.34 us (3%)
    all_gather x1, waiting for transfers between devices, local(): lax.all_gather(spectral, ('gz', 'grp'), axis=0, tiled=True)  62.4 us
    reduce_scatter x1, waiting for transfers between devices, local(): lax.psum_scatter(jnp.einsum('fpzx,xm->mfpz', tile_fields, columns, precis...  40.7 us
    all_gather x1, waiting for transfers between devices, local(): lax.all_gather(partial_sum, 'gx', axis=0, tiled=True)  36.3 us
    ppermute x6, waiting for transfers between devices, with_halo(): lax.ppermute(tail, axis, [(i, (i + 1) % count) for i in range(count)])  22.2 us
    ppermute x6, starting transfers between devices, with_halo(): lax.ppermute(head, axis, [((i + 1) % count, i) for i in range(count)])  16.7 us
    dot_general x1, matrix products, local(): jnp.einsum('mfpz,xm->fpzx', lax.all_gather(partial_sum, 'gx', axis=0, til...  15.7 us
    dot_general x1, matrix products, local(): jnp.einsum('fpzx,xm->mfpz', tile_fields, columns, precision=highest)  15.6 us
    all_to_all x1, waiting for transfers between devices, local(): lax.all_to_all(flat_lines, ('gz', 'grp'), split_axis=0, concat_axis=1, ti...  14.2 us
  transfers between devices with their start and end apart: 17, of which 14 were waited for; matrix products, arithmetic and copies ran while one was open for 1% of the time, Pallas kernels for 0%

commit v1 on v0

--- a/solution.py
+++ b/solution.py
@@ -155,12 +155,22 @@
         precision=highest,
     )
     columns = synth_x
-    filtered = jnp.einsum(
-        "mfpz,xm->fpzx",
-        lax.all_gather(partial_sum, "gx", axis=0, tiled=True),
-        columns,
-        precision=highest,
-    )
+    devices, index_2, rows = (lax.axis_size("gx"), lax.axis_index("gx"), partial_sum.shape[0])
+    upward = [(i_2, (i_2 + 1) % devices) for i_2 in range(devices)]
+    held, total = (partial_sum, None)
+    for turn in range(devices):
+        coming = lax.ppermute(held, "gx", upward) if turn < devices - 1 else None
+        update = jnp.einsum(
+            "mfpz,xm->fpzx",
+            held,
+            lax.dynamic_slice_in_dim(
+                columns, (index_2 - turn) % devices * rows, held.shape[0], axis=1
+            ),
+            precision=highest,
+        )
+        total = update if total is None else total + update
+        held = coming
+    filtered = total
     stresses = [
         filtered[3 + index] - filtered[first_idx] * filtered[second_idx]
         for index, (first_idx, second_idx) in enumerate(zip(pair_first, pair_second))

time: 304 us -> 286 us (0.941)
  waiting for transfers between devices: 189 us -> 179 us
  matrix products: 43.8 us -> 34.7 us
    all_gather x1 -> x0, waiting for transfers between devices: 36.3 us -> none  [local(): lax.all_gather(partial_sum, 'gx', axis=0, tiled=True)]
    ppermute x0 -> x3, waiting for transfers between devices: none -> 26.2 us  [local(): coming = lax.ppermute(held, 'gx', upward) if turn < devices - 1 else None]
    dot_general x1, matrix products: 15.6 us -> 9.82 us  [local(): jnp.einsum('fpzx,xm->mfpz', tile_fields, columns, precision=highest)]
    dot_general x1 -> x4, matrix products: 15.7 us -> 12.4 us  [local(): jnp.einsum('mfpz,xm->fpzx', held, lax.dynamic_slice_in_dim(columns, (inde...]
  transfers between devices with their start and end apart: 17 -> 19, of which waited for: 14 -> 16; matrix products, arithmetic and copies ran while one was open for 1% -> 5% of each run, Pallas kernels for 0% -> 0%
where the time goes in v1:
time: 286 us; the launch traced here: 281 us
  waiting for transfers between devices  179 us (63%)
  matrix products  34.7 us (12%)
  starting transfers between devices  31.3 us (11%)
  between operations  14.8 us (5%)
  other arithmetic  11 us (4%)
  local copies, waits for them, and re-layouts  9.85 us (3%)
    all_gather x1, waiting for transfers between devices, local(): lax.all_gather(spectral, ('gz', 'grp'), axis=0, tiled=True)  62.8 us
    reduce_scatter x1, waiting for transfers between devices, local(): lax.psum_scatter(jnp.einsum('fpzx,xm->mfpz', tile_fields, columns, precis...  40.7 us
    ppermute x3, waiting for transfers between devices, local(): coming = lax.ppermute(held, 'gx', upward) if turn < devices - 1 else None  26.2 us
    ppermute x6, waiting for transfers between devices, with_halo(): lax.ppermute(tail, axis, [(i, (i + 1) % count) for i in range(count)])  21.6 us
    ppermute x6, starting transfers between devices, with_halo(): lax.ppermute(head, axis, [((i + 1) % count, i) for i in range(count)])  17 us
    all_to_all x1, waiting for transfers between devices, local(): lax.all_to_all(flat_lines, ('gz', 'grp'), split_axis=0, concat_axis=1, ti...  14.2 us
    dot_general x4, matrix products, local(): jnp.einsum('mfpz,xm->fpzx', held, lax.dynamic_slice_in_dim(columns, (inde...  12.4 us
    dot_general x1, matrix products, local(): jnp.einsum('fpzx,xm->mfpz', tile_fields, columns, precision=highest)  9.82 us
  transfers between devices with their start and end apart: 19, of which 16 were waited for; matrix products, arithmetic and copies ran while one was open for 5% of the time, Pallas kernels for 0%

profile of v1, /device:TPU:0, one launch (start us, length us, event | category | flops | bytes accessed | tf_op | source)
XLA Modules:
  0.0 280.8 jit_solution(13616312574056113416)
XLA Ops:
  8.3 3.0 %collective-permute-start = (f32[3,3,1,512]{3,2,1,0:T(1,128)S(1)}, f32[3,3,1,512]{3,2,1,0:T(1,128)S(1)}, u32[]{:S(2)}, u32[]{:S(2)}) collective-permute-start(f32[3,3,1,512]{3,2,1,0:T(1,128)S(1)} %get-tuple-element.20), channel_id=1, source_target_pairs={{0,1},{1,2},{2,3},{3,4},{4,5},{5,6},{6,7},{7,0},{8,9},{9,10},{10,1... | collective-permute-start | bytes 55304 | tf_op jit(solution)/shard_map/ppermute | solution.py:24
  11.3 3.1 %collective-permute-start.1 = (f32[3,3,1,512]{3,2,1,0:T(1,128)S(1)}, f32[3,3,1,512]{3,2,1,0:T(1,128)S(1)}, u32[]{:S(2)}, u32[]{:S(2)}) collective-permute-start(f32[3,3,1,512]{3,2,1,0:T(1,128)S(1)} %get-tuple-element.21), channel_id=1, source_target_pairs={{1,0},{2,1},{3,2},{4,3},{5,4},{6,5},{7,6},{0,7},{9,8},{10,9},{11,1... | collective-permute-start | bytes 55304 | tf_op jit(solution)/shard_map/ppermute | solution.py:26
  16.4 1.7 collective-permute-start.2
  18.1 6.3 %collective-permute-done.3 = f32[3,3,66,1]{3,2,1,0:T(8,128)S(1)} collective-permute-done((f32[3,3,66,1]{3,2,1,0:T(8,128)S(1)}, f32[3,3,66,1]{3,2,1,0:T(8,128)S(1)}, u32[]{:S(2)}, u32[]{:S(2)}) %collective-permute-start.3) | collective-permute-done | bytes 2408 | tf_op jit(solution)/shard_map/ppermute | solution.py:24
  29.3 3.5 %collective-permute-start.5 = (f32[3,3,1,512]{3,2,1,0:T(1,128)S(1)}, f32[3,3,1,512]{3,2,1,0:T(1,128)S(1)}, u32[]{:S(2)}, u32[]{:S(2)}) collective-permute-start(f32[3,3,1,512]{3,2,1,0:T(1,128)S(1)} %get-tuple-element.17), channel_id=1, source_target_pairs={{1,0},{2,1},{3,2},{4,3},{5,4},{6,5},{7,6},{0,7},{9,8},{10,9},{11,1... | collective-permute-start | bytes 55304 | tf_op jit(solution)/shard_map/ppermute | solution.py:26
  32.8 1.8 collective-permute-done.4
  35.0 1.7 collective-permute-start.6
  36.7 6.2 %collective-permute-done.7 = f32[3,3,66,1]{3,2,1,0:T(8,128)S(1)} collective-permute-done((f32[3,3,66,1]{3,2,1,0:T(8,128)S(1)}, f32[3,3,66,1]{3,2,1,0:T(8,128)S(1)}, u32[]{:S(2)}, u32[]{:S(2)}) %collective-permute-start.7) | collective-permute-done | bytes 2408 | tf_op jit(solution)/shard_map/ppermute | solution.py:24
  46.1 4.8 %collective-permute-start.9 = (f32[3,3,1,512]{3,2,1,0:T(1,128)S(1)}, f32[3,3,1,512]{3,2,1,0:T(1,128)S(1)}, u32[]{:S(2)}, u32[]{:S(2)}) collective-permute-start(f32[3,3,1,512]{3,2,1,0:T(1,128)S(1)} %get-tuple-element.13), channel_id=1, source_target_pairs={{1,0},{2,1},{3,2},{4,3},{5,4},{6,5},{7,6},{0,7},{9,8},{10,9},{11,1... | collective-permute-start | bytes 55304 | tf_op jit(solution)/shard_map/ppermute | solution.py:26
  50.9 1.7 collective-permute-done.8
  52.8 2.2 collective-permute-start.10
  55.1 5.1 %collective-permute-done.11 = f32[3,3,66,1]{3,2,1,0:T(8,128)S(1)} collective-permute-done((f32[3,3,66,1]{3,2,1,0:T(8,128)S(1)}, f32[3,3,66,1]{3,2,1,0:T(8,128)S(1)}, u32[]{:S(2)}, u32[]{:S(2)}) %collective-permute-start.11) | collective-permute-done | bytes 2408 | tf_op jit(solution)/shard_map/ppermute | solution.py:24
  60.2 2.2 collective-permute-done.10
  65.3 9.8 %fusion.13 = f32[256,9,3,64]{3,0,2,1:T(8,128)} fusion(f32[9,3,64,512]{3,2,1,0:T(8,128)S(1)} %multiply_dynamic-update-slice_fusion, f32[256]{0:T(256)S(1)} %compare_select_fusion.4, s32[256]{0:T(256)S(1)} %add_select_fusion.4, s32[512]{0:T(512)S(1)} %iota_add_fusion, pred[256]{0:T(512)(128)(4,1)S(1)} %iota_compare_fusion), kind=kOutput, calls=%fused_computation.54 | convolution fusion | flops 2720006144 | bytes 5312768 | tf_op jit(solution)/shard_map/fpzx,xm->mfpz/dot_general | solution.py:124
  76.7 40.7 %reduce-scatter.2.cloned.1.call-done = f32[64,9,3,64]{3,0,2,1:T(8,128)} async-done(((f32[256,9,3,64]{3,0,2,1:T(8,128)}), f32[64,9,3,64]{3,0,2,1:T(8,128)}) %reduce-scatter.2.cloned.1.call-update) | async-done | bytes 442384 | tf_op jit(solution)/shard_map/reduce_scatter | solution.py:123
  117.4 1.8 copy.19
  120.8 5.7 %all-to-all-start = ((f32[8,216,64]{1,2,0:T(8,128)}), f32[8,216,64]{1,2,0:T(8,128)S(1)}, u32[]{:S(2)}, u32[]{:S(2)}) async-start(f32[8,216,64]{1,2,0:T(8,128)} %copy.20), calls=%async_computation.1 | async-start | bytes 1048576 | tf_op jit(solution)/shard_map/all_to_all | solution.py:134
  126.6 14.2 %all-to-all-done = f32[8,216,64]{1,2,0:T(8,128)S(1)} async-done(((f32[8,216,64]{1,2,0:T(8,128)}), f32[8,216,64]{1,2,0:T(8,128)S(1)}, u32[]{:S(2)}, u32[]{:S(2)}) %all-to-all-start) | async-done | bytes 442400 | tf_op jit(solution)/shard_map/all_to_all | solution.py:134
  140.8 4.6 %fusion.15 = f32[8,32,216]{2,1,0:T(8,128)} fusion(f32[216,512,1]{0,1,2:T(8,128)S(1)} %bitcast.69, f32[8,32]{1,0:T(8,128)S(1)} %fusion.84, s32[8,32]{1,0:T(8,128)S(1)} %add_select_fusion.3, pred[8,32]{1,0:T(8,128)(4,1)S(1)} %fusion.83), kind=kOutput, calls=%fused_computation.56 | convolution fusion | flops 341835776 | bytes 665856 | tf_op jit(solution)/shard_map/iz,zn->ni/dot_general | solution.py:138
  145.4 3.6 %all-to-all-start.1 = ((f32[8,32,216]{2,1,0:T(8,128)}), f32[8,32,216]{2,1,0:T(8,128)S(1)}, u32[]{:S(2)}, u32[]{:S(2)}) async-start(f32[8,32,216]{2,1,0:T(8,128)} %fusion.15), calls=%async_computation.2 | async-start | bytes 524288 | tf_op jit(solution)/shard_map/all_to_all | solution.py:139
  149.2 8.8 %all-to-all-done.1 = f32[8,32,216]{2,1,0:T(8,128)S(1)} async-done(((f32[8,32,216]{2,1,0:T(8,128)}), f32[8,32,216]{2,1,0:T(8,128)S(1)}, u32[]{:S(2)}, u32[]{:S(2)}) %all-to-all-start.1) | async-done | bytes 221216 | tf_op jit(solution)/shard_map/all_to_all | solution.py:139
  159.9 62.8 %all-gather.2.cloned.1.call-done = f32[256,64,9,3]{1,0,3,2:T(8,128)} async-done(((f32[32,64,9,3]{1,0,3,2:T(8,128)}), f32[256,64,9,3]{1,0,3,2:T(8,128)}) %all-gather.2.cloned.1.call-update) | async-done | bytes 1769488 | tf_op jit(solution)/shard_map/all_gather | solution.py:153
  222.7 7.9 %fusion.66 = f32[64,9,3,64]{3,0,2,1:T(8,128)S(1)} fusion(f32[256,64,9,3]{1,0,3,2:T(8,128)} %all-gather.2.cloned.1.call-done, s32[256]{0:T(256)S(1)} %add_select_fusion.4, s32[64]{0:T(128)S(1)} %iota_add_fusion.1, pred[256]{0:T(512)(128)(4,1)S(1)} %iota_compare_fusion), kind=kOutput, calls=%fused_computation.141 | convolution fusion | flops 339984384 | bytes 2213376 | tf_op jit(solution)/shard_map/nmfp,zn->mfpz/dot_general | solution.py:151
  230.7 12.5 %collective-permute-done.12 = f32[64,9,3,64]{3,0,2,1:T(8,128)S(1)} collective-permute-done((f32[64,9,3,64]{3,0,2,1:T(8,128)S(1)}, f32[64,9,3,64]{3,0,2,1:T(8,128)S(1)}, u32[]{:S(2)}, u32[]{:S(2)}) %collective-permute-start.12) | collective-permute-done | bytes 442400 | tf_op jit(solution)/shard_map/ppermute | solution.py:162
  243.1 2.1 sine_select_fusion
  245.4 3.0 %fusion.57 = f32[9,3,64,512]{3,2,1,0:T(8,128)S(1)} fusion(f32[64,9,3,64]{3,0,2,1:T(8,128)S(1)} %fusion.66, f32[512,256]{0,1:T(8,128)S(1)} %sine_select_fusion, s32[]{:T(128)S(6)} %select_n.187), kind=kOutput, calls=%fused_computation.127 | convolution fusion | flops 679477248 | bytes 4554756 | tf_op jit(solution)/shard_map/mfpz,xm->fpzx/dot_general | solution.py:163
  248.3 7.3 %collective-permute-done.13 = f32[64,9,3,64]{3,0,2,1:T(8,128)S(1)} collective-permute-done((f32[64,9,3,64]{3,0,2,1:T(8,128)S(1)}, f32[64,9,3,64]{3,0,2,1:T(8,128)S(1)}, u32[]{:S(2)}, u32[]{:S(2)}) %collective-permute-start.13) | collective-permute-done | bytes 442400 | tf_op jit(solution)/shard_map/ppermute | solution.py:162
  255.8 3.0 %fusion.55 = f32[9,3,64,512]{3,2,1,0:T(8,128)S(1)} fusion(f32[64,9,3,64]{3,0,2,1:T(8,128)S(1)} %collective-permute-done.12, f32[512,256]{0,1:T(8,128)S(1)} %sine_select_fusion, s32[]{:T(128)S(6)} %select_n.189), kind=kOutput, calls=%fused_computation.125 | convolution fusion | flops 679477248 | bytes 4554756 | tf_op jit(solution)/shard_map/mfpz,xm->fpzx/dot_general | solution.py:163
  258.8 3.0 %fusion.53 = f32[9,3,64,512]{3,2,1,0:T(8,128)S(1)} fusion(f32[64,9,3,64]{3,0,2,1:T(8,128)S(1)} %collective-permute-done.13, f32[512,256]{0,1:T(8,128)S(1)} %sine_select_fusion, s32[]{:T(128)S(6)} %select_n.191), kind=kOutput, calls=%fused_computation.123 | convolution fusion | flops 679477248 | bytes 4554756 | tf_op jit(solution)/shard_map/mfpz,xm->fpzx/dot_general | solution.py:163
  261.7 6.5 %collective-permute-done.14 = f32[64,9,3,64]{3,0,2,1:T(8,128)S(1)} collective-permute-done((f32[64,9,3,64]{3,0,2,1:T(8,128)S(1)}, f32[64,9,3,64]{3,0,2,1:T(8,128)S(1)}, u32[]{:S(2)}, u32[]{:S(2)}) %collective-permute-start.14) | collective-permute-done | bytes 442400 | tf_op jit(solution)/shard_map/ppermute | solution.py:162
  268.2 3.5 %add_add_fusion = f32[9,3,64,512]{3,2,1,0:T(8,128)S(1)} fusion(f32[9,3,64,512]{3,2,1,0:T(8,128)S(1)} %fusion.53, f32[9,3,64,512]{3,2,1,0:T(8,128)S(1)} %fusion.57, f32[9,3,64,512]{3,2,1,0:T(8,128)S(1)} %fusion.55, f32[64,9,3,64]{3,0,2,1:T(8,128)S(1)} %collective-permute-done.14, f32[512,256]{0,1:T(8,128)S(1)} %sine_select_fusion, s32[]{:T(128)S(6)} %select_n.193), kind=kOutput, calls=%fused_computation.2 | convolution fusion | flops 682131456 | bytes 15171588 | tf_op jit(solution)/shard_map/mfpz,xm->fpzx/dot_general | solution.py:163
  272.3 1.4 copy-done.2
  (87 shorter events, 20.4 us)
Async XLA Ops:
  7.2 9.0 %copy-start = (f32[3,3,64,512]{3,2,1,0:T(8,128)S(1)}, f32[3,3,64,512]{3,2,1,0:T(8,128)}, u32[]{:S(2)}) copy-start(f32[3,3,64,512]{3,2,1,0:T(8,128)} %param.4) | copy-start | bytes 3538948
  7.2 110.3 %reduce-scatter.2.cloned.1.call-start = ((), (), s32[]{:S(2)}) async-start(), calls=%async_computation.3 | async-start | bytes 4423680 | tf_op jit(solution)/shard_map/reduce_scatter | solution.py:123
  8.3 7.8 %collective-permute-start = (f32[3,3,1,512]{3,2,1,0:T(1,128)S(1)}, f32[3,3,1,512]{3,2,1,0:T(1,128)S(1)}, u32[]{:S(2)}, u32[]{:S(2)}) collective-permute-start(f32[3,3,1,512]{3,2,1,0:T(1,128)S(1)} %get-tuple-element.20), channel_id=1, source_target_pairs={{0,1},{1,2},{2,3},{3,4},{4,5},{5,6},{6,7},{7,0},{8,9},{9,10},{10,1... | collective-permute-start | bytes 55304 | tf_op jit(solution)/shard_map/ppermute | solution.py:24
  11.3 4.8 %collective-permute-start.1 = (f32[3,3,1,512]{3,2,1,0:T(1,128)S(1)}, f32[3,3,1,512]{3,2,1,0:T(1,128)S(1)}, u32[]{:S(2)}, u32[]{:S(2)}) collective-permute-start(f32[3,3,1,512]{3,2,1,0:T(1,128)S(1)} %get-tuple-element.21), channel_id=1, source_target_pairs={{1,0},{2,1},{3,2},{4,3},{5,4},{6,5},{7,6},{0,7},{9,8},{10,9},{11,1... | collective-permute-start | bytes 55304 | tf_op jit(solution)/shard_map/ppermute | solution.py:26
  16.3 8.1 %collective-permute-start.3 = (f32[3,3,66,1]{3,2,1,0:T(8,128)S(1)}, f32[3,3,66,1]{3,2,1,0:T(8,128)S(1)}, u32[]{:S(2)}, u32[]{:S(2)}) collective-permute-start(f32[3,3,66,1]{3,2,1,0:T(8,128)S(1)} %get-tuple-element.8), channel_id=1, source_target_pairs={{0,8},{8,16},{16,24},{24,0},{1,9},{9,17},{17,25},{25,1},{2,10},{10... | collective-permute-start | bytes 7136 | tf_op jit(solution)/shard_map/ppermute | solution.py:24
  16.4 9.3 %collective-permute-start.2 = (f32[3,3,66,1]{3,2,1,0:T(8,128)S(1)}, f32[3,3,66,1]{3,2,1,0:T(8,128)S(1)}, u32[]{:S(2)}, u32[]{:S(2)}) collective-permute-start(f32[3,3,66,1]{3,2,1,0:T(8,128)S(1)} %get-tuple-element.9), channel_id=1, source_target_pairs={{8,0},{16,8},{24,16},{0,24},{9,1},{17,9},{25,17},{1,25},{10,2},{18... | collective-permute-start | bytes 7136 | tf_op jit(solution)/shard_map/ppermute | solution.py:26
  26.9 0.7 copy-start.4
  27.9 8.7 %copy-start.3 = (f32[3]{0:T(128)S(1)}, f32[3]{0:T(128)}, u32[]{:S(2)}) copy-start(f32[3]{0:T(128)} %param.5) | copy-start | bytes 40
  28.0 6.7 %collective-permute-start.4 = (f32[3,3,1,512]{3,2,1,0:T(1,128)S(1)}, f32[3,3,1,512]{3,2,1,0:T(1,128)S(1)}, u32[]{:S(2)}, u32[]{:S(2)}) collective-permute-start(f32[3,3,1,512]{3,2,1,0:T(1,128)S(1)} %get-tuple-element.16), channel_id=1, source_target_pairs={{0,1},{1,2},{2,3},{3,4},{4,5},{5,6},{6,7},{7,0},{8,9},{9,10},{10,1... | collective-permute-start | bytes 55304 | tf_op jit(solution)/shard_map/ppermute | solution.py:24
  29.3 5.4 %collective-permute-start.5 = (f32[3,3,1,512]{3,2,1,0:T(1,128)S(1)}, f32[3,3,1,512]{3,2,1,0:T(1,128)S(1)}, u32[]{:S(2)}, u32[]{:S(2)}) collective-permute-start(f32[3,3,1,512]{3,2,1,0:T(1,128)S(1)} %get-tuple-element.17), channel_id=1, source_target_pairs={{1,0},{2,1},{3,2},{4,3},{5,4},{6,5},{7,6},{0,7},{9,8},{10,9},{11,1... | collective-permute-start | bytes 55304 | tf_op jit(solution)/shard_map/ppermute | solution.py:26
  34.8 8.1 %collective-permute-start.7 = (f32[3,3,66,1]{3,2,1,0:T(8,128)S(1)}, f32[3,3,66,1]{3,2,1,0:T(8,128)S(1)}, u32[]{:S(2)}, u32[]{:S(2)}) collective-permute-start(f32[3,3,66,1]{3,2,1,0:T(8,128)S(1)} %get-tuple-element.6), channel_id=1, source_target_pairs={{0,8},{8,16},{16,24},{24,0},{1,9},{9,17},{17,25},{25,1},{2,10},{10... | collective-permute-start | bytes 7136 | tf_op jit(solution)/shard_map/ppermute | solution.py:24
  35.0 9.2 %collective-permute-start.6 = (f32[3,3,66,1]{3,2,1,0:T(8,128)S(1)}, f32[3,3,66,1]{3,2,1,0:T(8,128)S(1)}, u32[]{:S(2)}, u32[]{:S(2)}) collective-permute-start(f32[3,3,66,1]{3,2,1,0:T(8,128)S(1)} %get-tuple-element.7), channel_id=1, source_target_pairs={{8,0},{16,8},{24,16},{0,24},{9,1},{17,9},{25,17},{1,25},{10,2},{18... | collective-permute-start | bytes 7136 | tf_op jit(solution)/shard_map/ppermute | solution.py:26
  46.1 6.5 %collective-permute-start.8 = (f32[3,3,1,512]{3,2,1,0:T(1,128)S(1)}, f32[3,3,1,512]{3,2,1,0:T(1,128)S(1)}, u32[]{:S(2)}, u32[]{:S(2)}) collective-permute-start(f32[3,3,1,512]{3,2,1,0:T(1,128)S(1)} %get-tuple-element.12), channel_id=1, source_target_pairs={{0,1},{1,2},{2,3},{3,4},{4,5},{5,6},{6,7},{7,0},{8,9},{9,10},{10,1... | collective-permute-start | bytes 55304 | tf_op jit(solution)/shard_map/ppermute | solution.py:24
  46.1 6.5 %collective-permute-start.9 = (f32[3,3,1,512]{3,2,1,0:T(1,128)S(1)}, f32[3,3,1,512]{3,2,1,0:T(1,128)S(1)}, u32[]{:S(2)}, u32[]{:S(2)}) collective-permute-start(f32[3,3,1,512]{3,2,1,0:T(1,128)S(1)} %get-tuple-element.13), channel_id=1, source_target_pairs={{1,0},{2,1},{3,2},{4,3},{5,4},{6,5},{7,6},{0,7},{9,8},{10,9},{11,1... | collective-permute-start | bytes 55304 | tf_op jit(solution)/shard_map/ppermute | solution.py:26
  52.8 7.4 %collective-permute-start.11 = (f32[3,3,66,1]{3,2,1,0:T(8,128)S(1)}, f32[3,3,66,1]{3,2,1,0:T(8,128)S(1)}, u32[]{:S(2)}, u32[]{:S(2)}) collective-permute-start(f32[3,3,66,1]{3,2,1,0:T(8,128)S(1)} %get-tuple-element.4), channel_id=1, source_target_pairs={{0,8},{8,16},{16,24},{24,0},{1,9},{9,17},{17,25},{25,1},{2,10},{10... | collective-permute-start | bytes 7136 | tf_op jit(solution)/shard_map/ppermute | solution.py:24
  52.8 9.6 %collective-permute-start.10 = (f32[3,3,66,1]{3,2,1,0:T(8,128)S(1)}, f32[3,3,66,1]{3,2,1,0:T(8,128)S(1)}, u32[]{:S(2)}, u32[]{:S(2)}) collective-permute-start(f32[3,3,66,1]{3,2,1,0:T(8,128)S(1)} %get-tuple-element.5), channel_id=1, source_target_pairs={{8,0},{16,8},{24,16},{0,24},{9,1},{17,9},{25,17},{1,25},{10,2},{18... | collective-permute-start | bytes 7136 | tf_op jit(solution)/shard_map/ppermute | solution.py:26
  64.2 1.0 copy-start.1
  119.6 6.9 %copy-start.5 = (s32[3,2]{0,1:T(2,128)S(1)}, s32[3,2]{0,1:T(2,128)}, u32[]{:S(2)}) copy-start(s32[3,2]{0,1:T(2,128)} %param.7) | copy-start | bytes 76
  120.8 20.0 %all-to-all-start = ((f32[8,216,64]{1,2,0:T(8,128)}), f32[8,216,64]{1,2,0:T(8,128)S(1)}, u32[]{:S(2)}, u32[]{:S(2)}) async-start(f32[8,216,64]{1,2,0:T(8,128)} %copy.20), calls=%async_computation.1 | async-start | bytes 1048576 | tf_op jit(solution)/shard_map/all_to_all | solution.py:134
  145.4 12.7 %all-to-all-start.1 = ((f32[8,32,216]{2,1,0:T(8,128)}), f32[8,32,216]{2,1,0:T(8,128)S(1)}, u32[]{:S(2)}, u32[]{:S(2)}) async-start(f32[8,32,216]{2,1,0:T(8,128)} %fusion.15), calls=%async_computation.2 | async-start | bytes 524288 | tf_op jit(solution)/shard_map/all_to_all | solution.py:139
  149.0 73.7 %all-gather.2.cloned.1.call-start = ((), (), s32[]{:S(2)}) async-start(), calls=%async_computation.4 | async-start | bytes 3981312 | tf_op jit(solution)/shard_map/all_gather | solution.py:153
  230.6 12.5 %collective-permute-start.12 = (f32[64,9,3,64]{3,0,2,1:T(8,128)S(1)}, f32[64,9,3,64]{3,0,2,1:T(8,128)S(1)}, u32[]{:S(2)}, u32[]{:S(2)}) collective-permute-start(f32[64,9,3,64]{3,0,2,1:T(8,128)S(1)} %fusion.66), channel_id=1, source_target_pairs={{0,8},{8,16},{16,24},{24,0},{1,9},{9,17},{17,25},{25,1},{2,10},{10... | collective-permute-start | bytes 1327112 | tf_op jit(solution)/shard_map/ppermute | solution.py:162
  243.1 12.5 %collective-permute-start.13 = (f32[64,9,3,64]{3,0,2,1:T(8,128)S(1)}, f32[64,9,3,64]{3,0,2,1:T(8,128)S(1)}, u32[]{:S(2)}, u32[]{:S(2)}) collective-permute-start(f32[64,9,3,64]{3,0,2,1:T(8,128)S(1)} %collective-permute-done.12), channel_id=1, source_target_pairs={{0,8},{8,16},{16,24},{24,0},{1,9},{9,17},{17,25},{25,1},{2,10},{10... | collective-permute-start | bytes 1327112 | tf_op jit(solution)/shard_map/ppermute | solution.py:162
  255.6 12.7 %collective-permute-start.14 = (f32[64,9,3,64]{3,0,2,1:T(8,128)S(1)}, f32[64,9,3,64]{3,0,2,1:T(8,128)S(1)}, u32[]{:S(2)}, u32[]{:S(2)}) collective-permute-start(f32[64,9,3,64]{3,0,2,1:T(8,128)S(1)} %collective-permute-done.13), channel_id=1, source_target_pairs={{0,8},{8,16},{16,24},{24,0},{1,9},{9,17},{17,25},{25,1},{2,10},{10... | collective-permute-start | bytes 1327112 | tf_op jit(solution)/shard_map/ppermute | solution.py:162
  272.3 1.4 copy-start.2
Sparse Core Ops, SparseCore 0:
  75.2 42.1 reduce-scatter.1
  160.0 62.6 all-gather.1
